TPU v7x, 256 devices: a whole 4x4x8 slice. The times are simulated.
256 devices in a mesh: blk: 16 (over y_hi, z), grp: 16 (over x, y_lo, core).
Axes of the slice: x: 4, y: 4 (y_hi: 2, y_lo: 2; y = y_hi * 2 + y_lo), z: 8, core: 2. Of those that a mesh axis runs over, the one named last changes fastest.
Arguments:
- history: bfloat16 [96, 32, 32768], P(None, None, ('blk', 'grp')), may hold values from -6 to 6
- delays: int32 [256, 256], P(('blk', 'grp')), may hold values from 0 to 92
- offsets: int32 [256, 256], P(('blk', 'grp')), may hold values from 0 to 7
- kernel: bfloat16 [32768, 32768], P(('blk', 'grp')), may hold values from -0.125 to 0.125
- incident: float32 [32, 32768], P(None, ('blk', 'grp')), may hold values from -6 to 6
- inverse: float32 [32768, 128], P(('blk', 'grp'))
Outputs:
- current: float32 [32, 32768], P(None, ('blk', 'grp'))
All inputs are finite; a program needn't handle non-finite values.
Results may differ from a plain program's by a relative error of at most 0.0019.
Values may be sent and summed in bfloat16 or wider, within the bound.
A program may use at most 64 MiB of HBM per device.

v0:
```python
import jax
import jax.numpy as jnp
import numpy as np
from jax import lax
from jax.sharding import PartitionSpec as P

ORDER = 4
FRAC = 8


def passed_along(x, axis, by):
    length = lax.axis_size(axis)
    return lax.ppermute(x, axis, [(i, (i + by) % length) for i in range(length)])


def weight_table():
    fractions = np.arange(FRAC) / FRAC
    node_list = np.arange(ORDER) - (ORDER // 2 - 1)
    lagrange = np.ones((FRAC, ORDER))
    for column in range(ORDER):
        for partner in range(ORDER):
            if partner != column:
                lagrange[:, column] = (
                    lagrange[:, column]
                    * (fractions - node_list[partner])
                    / (node_list[column] - node_list[partner])
                )
    return jnp.asarray(lagrange, jnp.float32)


def retarded(history_block, delay_row, offset_row, lagrange):
    window_rows = delay_row[:, None] + jnp.arange(ORDER, dtype=jnp.int32)[None, :]
    windows = jnp.take(history_block, window_rows, axis=0).astype(jnp.float32)
    chooser = (offset_row[:, None] == jnp.arange(FRAC, dtype=jnp.int32)[None, :]).astype(
        jnp.float32
    )
    weights = jnp.dot(chooser, lagrange, precision=lax.Precision.HIGHEST)
    slices = jnp.einsum("mp,mpqr->mqr", weights, windows, precision=lax.Precision.HIGHEST)
    return slices.astype(jnp.bfloat16)


def per_device(history, delays, offsets, kernel, incident, inverse):
    lagrange = weight_table()
    row_count = history.shape[2]
    excite_count = history.shape[1]
    group_count = lax.axis_size("grp")
    cycle_count = lax.axis_size("blk")
    here_blk = lax.axis_index("blk")
    kernel_grid = kernel.reshape(row_count, cycle_count * group_count, row_count)
    initial = jnp.zeros((excite_count, row_count), jnp.float32)
    group_obs = here_blk * group_count + jnp.arange(group_count, dtype=jnp.int32)

    def gather_source(summed, held, source_blk):
        history_block, delay_local, offset_local = held
        delay_row = jnp.take(delay_local[0], group_obs)
        offset_row = jnp.take(offset_local[0], group_obs)
        slices = retarded(history_block, delay_row, offset_row, lagrange)
        kernel_tiles = lax.dynamic_slice_in_dim(
            kernel_grid, source_blk * group_count, group_count, 1
        )
        return summed + lax.dot_general(
            lax.all_to_all(slices, "grp", split_axis=0, concat_axis=0, tiled=True),
            kernel_tiles,
            (((0, 2), (1, 2)), ((), ())),
            preferred_element_type=jnp.float32,
        )

    own_held = (history, delays, offsets)
    summed = gather_source(initial, own_held, here_blk)

    def one_turn(turn_index, carried):
        held, summed_now = carried
        held = passed_along((held[0], held[1], held[2]), "blk", 1)
        summed_now = gather_source(summed_now, held, (here_blk - turn_index) % cycle_count)
        return (held, summed_now)

    held_last, summed = lax.fori_loop(1, cycle_count, one_turn, (own_held, summed))
    rhs_field = incident - summed
    return lax.dot_general(
        rhs_field, inverse, (((1,), (1,)), ((), ())), precision=lax.Precision.HIGHEST
    )


def solution(mesh):
    return jax.shard_map(
        per_device,
        mesh=mesh,
        in_specs=(
            P(None, None, ("blk", "grp")),
            P(("blk", "grp"), None),
            P(("blk", "grp"), None),
            P(("blk", "grp"), None),
            P(None, ("blk", "grp")),
            P(("blk", "grp"), None),
        ),
        out_specs=P(None, ("blk", "grp")),
        check_vma=False,
    )
```

profile of v0, /device:TPU:1, one launch (start us, length us, event | category | flops | bytes accessed | tf_op | source)
XLA Modules:
  0.0 602.5 jit_solution(10681435631261862077)
XLA Ops:
  7.5 6.8 %all-to-all-start.1 = ((bf16[16,32,128]{2,1,0:T(8,128)(2,1)}), bf16[16,32,128]{2,1,0:T(8,128)(2,1)S(1)}, u32[]{:S(2)}, u32[]{:S(2)}) async-start(bf16[16,32,128]{2,1,0:T(8,128)(2,1)} %convert_element_type.21), calls=%async_computation.1 | async-start | bytes 262144 | tf_op jit(solution)/shard_map/all_to_all | solution.py:62
  14.3 12.0 %copy.8 = bf16[128,32768]{0,1:T(8,128)(2,1)} copy(bf16[128,32768]{1,0:T(8,128)(2,1)} %param.16) | data formatting | bytes 16777216 | tf_op args[3]
  27.6 574.1 %while.23 = (s32[]{:T(128)}, bf16[96,32,128]{2,1,0:T(8,128)(2,1)S(1)}, s32[1,256]{1,0:T(1,128)S(1)}, s32[1,256]{1,0:T(1,128)S(1)}, f32[32,128]{1,0:T(8,128)S(1)}...) while((s32[]{:T(128)}, ...), condition=%wide.region_1.4_spmd.clone.clone, body=%wide.region_0.3_spmd.sunk.clone.clone.sunk | while | flops 20264080 | bytes 9100692 | solution.py:77
  37.4 16.1 %collective-permute-done.2 = s32[1,256]{1,0:T(1,128)S(1)} collective-permute-done((s32[1,256]{1,0:T(1,128)S(1)}, s32[1,256]{1,0:T(1,128)S(1)}, u32[]{:S(2)}, u32[]{:S(2)}) %collective-permute-start.2) | collective-permute-done | bytes 1056 | tf_op jit(solution)/shard_map/while/body/eval_jaxpr/ppermute | solution.py:13
  76.7 15.5 %collective-permute-done.2 = s32[1,256]{1,0:T(1,128)S(1)} collective-permute-done((s32[1,256]{1,0:T(1,128)S(1)}, s32[1,256]{1,0:T(1,128)S(1)}, u32[]{:S(2)}, u32[]{:S(2)}) %collective-permute-start.2) | collective-permute-done | bytes 1056 | tf_op jit(solution)/shard_map/while/body/eval_jaxpr/ppermute | solution.py:13
  100.4 6.1 %all-to-all-done = bf16[16,32,128]{2,1,0:T(8,128)(2,1)S(1)} async-done(((bf16[16,32,128]{2,1,0:T(8,128)(2,1)}), bf16[16,32,128]{2,1,0:T(8,128)(2,1)S(1)}, u32[]{:S(2)}, u32[]{:S(2)}) %all-to-all-start) | async-done | bytes 131104 | tf_op jit(solution)/shard_map/while/body/eval_jaxpr/all_to_all | solution.py:62
  114.7 15.5 %collective-permute-done.2 = s32[1,256]{1,0:T(1,128)S(1)} collective-permute-done((s32[1,256]{1,0:T(1,128)S(1)}, s32[1,256]{1,0:T(1,128)S(1)}, u32[]{:S(2)}, u32[]{:S(2)}) %collective-permute-start.2) | collective-permute-done | bytes 1056 | tf_op jit(solution)/shard_map/while/body/eval_jaxpr/ppermute | solution.py:13
  152.7 15.5 %collective-permute-done.2 = s32[1,256]{1,0:T(1,128)S(1)} collective-permute-done((s32[1,256]{1,0:T(1,128)S(1)}, s32[1,256]{1,0:T(1,128)S(1)}, u32[]{:S(2)}, u32[]{:S(2)}) %collective-permute-start.2) | collective-permute-done | bytes 1056 | tf_op jit(solution)/shard_map/while/body/eval_jaxpr/ppermute | solution.py:13
  176.3 6.1 %all-to-all-done = bf16[16,32,128]{2,1,0:T(8,128)(2,1)S(1)} async-done(((bf16[16,32,128]{2,1,0:T(8,128)(2,1)}), bf16[16,32,128]{2,1,0:T(8,128)(2,1)S(1)}, u32[]{:S(2)}, u32[]{:S(2)}) %all-to-all-start) | async-done | bytes 131104 | tf_op jit(solution)/shard_map/while/body/eval_jaxpr/all_to_all | solution.py:62
  190.7 15.5 %collective-permute-done.2 = s32[1,256]{1,0:T(1,128)S(1)} collective-permute-done((s32[1,256]{1,0:T(1,128)S(1)}, s32[1,256]{1,0:T(1,128)S(1)}, u32[]{:S(2)}, u32[]{:S(2)}) %collective-permute-start.2) | collective-permute-done | bytes 1056 | tf_op jit(solution)/shard_map/while/body/eval_jaxpr/ppermute | solution.py:13
  214.3 6.1 %all-to-all-done = bf16[16,32,128]{2,1,0:T(8,128)(2,1)S(1)} async-done(((bf16[16,32,128]{2,1,0:T(8,128)(2,1)}), bf16[16,32,128]{2,1,0:T(8,128)(2,1)S(1)}, u32[]{:S(2)}, u32[]{:S(2)}) %all-to-all-start) | async-done | bytes 131104 | tf_op jit(solution)/shard_map/while/body/eval_jaxpr/all_to_all | solution.py:62
  228.7 15.5 %collective-permute-done.2 = s32[1,256]{1,0:T(1,128)S(1)} collective-permute-done((s32[1,256]{1,0:T(1,128)S(1)}, s32[1,256]{1,0:T(1,128)S(1)}, u32[]{:S(2)}, u32[]{:S(2)}) %collective-permute-start.2) | collective-permute-done | bytes 1056 | tf_op jit(solution)/shard_map/while/body/eval_jaxpr/ppermute | solution.py:13
  266.7 15.5 %collective-permute-done.2 = s32[1,256]{1,0:T(1,128)S(1)} collective-permute-done((s32[1,256]{1,0:T(1,128)S(1)}, s32[1,256]{1,0:T(1,128)S(1)}, u32[]{:S(2)}, u32[]{:S(2)}) %collective-permute-start.2) | collective-permute-done | bytes 1056 | tf_op jit(solution)/shard_map/while/body/eval_jaxpr/ppermute | solution.py:13
  290.3 6.1 %all-to-all-done = bf16[16,32,128]{2,1,0:T(8,128)(2,1)S(1)} async-done(((bf16[16,32,128]{2,1,0:T(8,128)(2,1)}), bf16[16,32,128]{2,1,0:T(8,128)(2,1)S(1)}, u32[]{:S(2)}, u32[]{:S(2)}) %all-to-all-start) | async-done | bytes 131104 | tf_op jit(solution)/shard_map/while/body/eval_jaxpr/all_to_all | solution.py:62
  304.7 15.5 %collective-permute-done.2 = s32[1,256]{1,0:T(1,128)S(1)} collective-permute-done((s32[1,256]{1,0:T(1,128)S(1)}, s32[1,256]{1,0:T(1,128)S(1)}, u32[]{:S(2)}, u32[]{:S(2)}) %collective-permute-start.2) | collective-permute-done | bytes 1056 | tf_op jit(solution)/shard_map/while/body/eval_jaxpr/ppermute | solution.py:13
  328.3 6.1 %all-to-all-done = bf16[16,32,128]{2,1,0:T(8,128)(2,1)S(1)} async-done(((bf16[16,32,128]{2,1,0:T(8,128)(2,1)}), bf16[16,32,128]{2,1,0:T(8,128)(2,1)S(1)}, u32[]{:S(2)}, u32[]{:S(2)}) %all-to-all-start) | async-done | bytes 131104 | tf_op jit(solution)/shard_map/while/body/eval_jaxpr/all_to_all | solution.py:62
  342.7 15.5 %collective-permute-done.2 = s32[1,256]{1,0:T(1,128)S(1)} collective-permute-done((s32[1,256]{1,0:T(1,128)S(1)}, s32[1,256]{1,0:T(1,128)S(1)}, u32[]{:S(2)}, u32[]{:S(2)}) %collective-permute-start.2) | collective-permute-done | bytes 1056 | tf_op jit(solution)/shard_map/while/body/eval_jaxpr/ppermute | solution.py:13
  366.3 6.1 %all-to-all-done = bf16[16,32,128]{2,1,0:T(8,128)(2,1)S(1)} async-done(((bf16[16,32,128]{2,1,0:T(8,128)(2,1)}), bf16[16,32,128]{2,1,0:T(8,128)(2,1)S(1)}, u32[]{:S(2)}, u32[]{:S(2)}) %all-to-all-start) | async-done | bytes 131104 | tf_op jit(solution)/shard_map/while/body/eval_jaxpr/all_to_all | solution.py:62
  380.7 15.5 %collective-permute-done.2 = s32[1,256]{1,0:T(1,128)S(1)} collective-permute-done((s32[1,256]{1,0:T(1,128)S(1)}, s32[1,256]{1,0:T(1,128)S(1)}, u32[]{:S(2)}, u32[]{:S(2)}) %collective-permute-start.2) | collective-permute-done | bytes 1056 | tf_op jit(solution)/shard_map/while/body/eval_jaxpr/ppermute | solution.py:13
  418.7 15.5 %collective-permute-done.2 = s32[1,256]{1,0:T(1,128)S(1)} collective-permute-done((s32[1,256]{1,0:T(1,128)S(1)}, s32[1,256]{1,0:T(1,128)S(1)}, u32[]{:S(2)}, u32[]{:S(2)}) %collective-permute-start.2) | collective-permute-done | bytes 1056 | tf_op jit(solution)/shard_map/while/body/eval_jaxpr/ppermute | solution.py:13
  456.7 15.5 %collective-permute-done.2 = s32[1,256]{1,0:T(1,128)S(1)} collective-permute-done((s32[1,256]{1,0:T(1,128)S(1)}, s32[1,256]{1,0:T(1,128)S(1)}, u32[]{:S(2)}, u32[]{:S(2)}) %collective-permute-start.2) | collective-permute-done | bytes 1056 | tf_op jit(solution)/shard_map/while/body/eval_jaxpr/ppermute | solution.py:13
  494.6 15.5 %collective-permute-done.2 = s32[1,256]{1,0:T(1,128)S(1)} collective-permute-done((s32[1,256]{1,0:T(1,128)S(1)}, s32[1,256]{1,0:T(1,128)S(1)}, u32[]{:S(2)}, u32[]{:S(2)}) %collective-permute-start.2) | collective-permute-done | bytes 1056 | tf_op jit(solution)/shard_map/while/body/eval_jaxpr/ppermute | solution.py:13
  532.6 15.5 %collective-permute-done.2 = s32[1,256]{1,0:T(1,128)S(1)} collective-permute-done((s32[1,256]{1,0:T(1,128)S(1)}, s32[1,256]{1,0:T(1,128)S(1)}, u32[]{:S(2)}, u32[]{:S(2)}) %collective-permute-start.2) | collective-permute-done | bytes 1056 | tf_op jit(solution)/shard_map/while/body/eval_jaxpr/ppermute | solution.py:13
  570.6 15.5 %collective-permute-done.2 = s32[1,256]{1,0:T(1,128)S(1)} collective-permute-done((s32[1,256]{1,0:T(1,128)S(1)}, s32[1,256]{1,0:T(1,128)S(1)}, u32[]{:S(2)}, u32[]{:S(2)}) %collective-permute-start.2) | collective-permute-done | bytes 1056 | tf_op jit(solution)/shard_map/while/body/eval_jaxpr/ppermute | solution.py:13
  (410 shorter events, 312.0 us)
Async XLA Ops:
  29.3 25.2 %collective-permute-start = (bf16[96,32,128]{2,1,0:T(8,128)(2,1)S(1)}, bf16[96,32,128]{2,1,0:T(8,128)(2,1)S(1)}, u32[]{:S(2)}, u32[]{:S(2)}) collective-permute-start(bf16[96,32,128]{2,1,0:T(8,128)(2,1)S(1)} %get-tuple-element.365), channel_id=1, source_target_pairs={{0,16},{16,32},{32,48},{48,64},{64,80},{80,96},{96,112},{112,128},... | collective-permute-start | bytes 2359304 | tf_op jit(solution)/shard_map/while/body/eval_jaxpr/ppermute | solution.py:13
  30.9 22.6 %collective-permute-start.2 = (s32[1,256]{1,0:T(1,128)S(1)}, s32[1,256]{1,0:T(1,128)S(1)}, u32[]{:S(2)}, u32[]{:S(2)}) collective-permute-start(s32[1,256]{1,0:T(1,128)S(1)} %get-tuple-element.367), channel_id=1, source_target_pairs={{0,16},{16,32},{32,48},{48,64},{64,80},{80,96},{96,112},{112,128},... | collective-permute-start | bytes 3080 | tf_op jit(solution)/shard_map/while/body/eval_jaxpr/ppermute | solution.py:13
  69.8 23.3 %collective-permute-start = (bf16[96,32,128]{2,1,0:T(8,128)(2,1)S(1)}, bf16[96,32,128]{2,1,0:T(8,128)(2,1)S(1)}, u32[]{:S(2)}, u32[]{:S(2)}) collective-permute-start(bf16[96,32,128]{2,1,0:T(8,128)(2,1)S(1)} %get-tuple-element.365), channel_id=1, source_target_pairs={{0,16},{16,32},{32,48},{48,64},{64,80},{80,96},{96,112},{112,128},... | collective-permute-start | bytes 2359304 | tf_op jit(solution)/shard_map/while/body/eval_jaxpr/ppermute | solution.py:13
  69.9 22.3 %collective-permute-start.2 = (s32[1,256]{1,0:T(1,128)S(1)}, s32[1,256]{1,0:T(1,128)S(1)}, u32[]{:S(2)}, u32[]{:S(2)}) collective-permute-start(s32[1,256]{1,0:T(1,128)S(1)} %get-tuple-element.367), channel_id=1, source_target_pairs={{0,16},{16,32},{32,48},{48,64},{64,80},{80,96},{96,112},{112,128},... | collective-permute-start | bytes 3080 | tf_op jit(solution)/shard_map/while/body/eval_jaxpr/ppermute | solution.py:13
  107.8 23.3 %collective-permute-start = (bf16[96,32,128]{2,1,0:T(8,128)(2,1)S(1)}, bf16[96,32,128]{2,1,0:T(8,128)(2,1)S(1)}, u32[]{:S(2)}, u32[]{:S(2)}) collective-permute-start(bf16[96,32,128]{2,1,0:T(8,128)(2,1)S(1)} %get-tuple-element.365), channel_id=1, source_target_pairs={{0,16},{16,32},{32,48},{48,64},{64,80},{80,96},{96,112},{112,128},... | collective-permute-start | bytes 2359304 | tf_op jit(solution)/shard_map/while/body/eval_jaxpr/ppermute | solution.py:13
  107.9 22.3 %collective-permute-start.2 = (s32[1,256]{1,0:T(1,128)S(1)}, s32[1,256]{1,0:T(1,128)S(1)}, u32[]{:S(2)}, u32[]{:S(2)}) collective-permute-start(s32[1,256]{1,0:T(1,128)S(1)} %get-tuple-element.367), channel_id=1, source_target_pairs={{0,16},{16,32},{32,48},{48,64},{64,80},{80,96},{96,112},{112,128},... | collective-permute-start | bytes 3080 | tf_op jit(solution)/shard_map/while/body/eval_jaxpr/ppermute | solution.py:13
  145.8 23.3 %collective-permute-start = (bf16[96,32,128]{2,1,0:T(8,128)(2,1)S(1)}, bf16[96,32,128]{2,1,0:T(8,128)(2,1)S(1)}, u32[]{:S(2)}, u32[]{:S(2)}) collective-permute-start(bf16[96,32,128]{2,1,0:T(8,128)(2,1)S(1)} %get-tuple-element.365), channel_id=1, source_target_pairs={{0,16},{16,32},{32,48},{48,64},{64,80},{80,96},{96,112},{112,128},... | collective-permute-start | bytes 2359304 | tf_op jit(solution)/shard_map/while/body/eval_jaxpr/ppermute | solution.py:13
  145.9 22.3 %collective-permute-start.2 = (s32[1,256]{1,0:T(1,128)S(1)}, s32[1,256]{1,0:T(1,128)S(1)}, u32[]{:S(2)}, u32[]{:S(2)}) collective-permute-start(s32[1,256]{1,0:T(1,128)S(1)} %get-tuple-element.367), channel_id=1, source_target_pairs={{0,16},{16,32},{32,48},{48,64},{64,80},{80,96},{96,112},{112,128},... | collective-permute-start | bytes 3080 | tf_op jit(solution)/shard_map/while/body/eval_jaxpr/ppermute | solution.py:13
  183.8 23.3 %collective-permute-start = (bf16[96,32,128]{2,1,0:T(8,128)(2,1)S(1)}, bf16[96,32,128]{2,1,0:T(8,128)(2,1)S(1)}, u32[]{:S(2)}, u32[]{:S(2)}) collective-permute-start(bf16[96,32,128]{2,1,0:T(8,128)(2,1)S(1)} %get-tuple-element.365), channel_id=1, source_target_pairs={{0,16},{16,32},{32,48},{48,64},{64,80},{80,96},{96,112},{112,128},... | collective-permute-start | bytes 2359304 | tf_op jit(solution)/shard_map/while/body/eval_jaxpr/ppermute | solution.py:13
  183.9 22.3 %collective-permute-start.2 = (s32[1,256]{1,0:T(1,128)S(1)}, s32[1,256]{1,0:T(1,128)S(1)}, u32[]{:S(2)}, u32[]{:S(2)}) collective-permute-start(s32[1,256]{1,0:T(1,128)S(1)} %get-tuple-element.367), channel_id=1, source_target_pairs={{0,16},{16,32},{32,48},{48,64},{64,80},{80,96},{96,112},{112,128},... | collective-permute-start | bytes 3080 | tf_op jit(solution)/shard_map/while/body/eval_jaxpr/ppermute | solution.py:13
  221.8 23.3 %collective-permute-start = (bf16[96,32,128]{2,1,0:T(8,128)(2,1)S(1)}, bf16[96,32,128]{2,1,0:T(8,128)(2,1)S(1)}, u32[]{:S(2)}, u32[]{:S(2)}) collective-permute-start(bf16[96,32,128]{2,1,0:T(8,128)(2,1)S(1)} %get-tuple-element.365), channel_id=1, source_target_pairs={{0,16},{16,32},{32,48},{48,64},{64,80},{80,96},{96,112},{112,128},... | collective-permute-start | bytes 2359304 | tf_op jit(solution)/shard_map/while/body/eval_jaxpr/ppermute | solution.py:13
  221.9 22.3 %collective-permute-start.2 = (s32[1,256]{1,0:T(1,128)S(1)}, s32[1,256]{1,0:T(1,128)S(1)}, u32[]{:S(2)}, u32[]{:S(2)}) collective-permute-start(s32[1,256]{1,0:T(1,128)S(1)} %get-tuple-element.367), channel_id=1, source_target_pairs={{0,16},{16,32},{32,48},{48,64},{64,80},{80,96},{96,112},{112,128},... | collective-permute-start | bytes 3080 | tf_op jit(solution)/shard_map/while/body/eval_jaxpr/ppermute | solution.py:13
  259.8 23.3 %collective-permute-start = (bf16[96,32,128]{2,1,0:T(8,128)(2,1)S(1)}, bf16[96,32,128]{2,1,0:T(8,128)(2,1)S(1)}, u32[]{:S(2)}, u32[]{:S(2)}) collective-permute-start(bf16[96,32,128]{2,1,0:T(8,128)(2,1)S(1)} %get-tuple-element.365), channel_id=1, source_target_pairs={{0,16},{16,32},{32,48},{48,64},{64,80},{80,96},{96,112},{112,128},... | collective-permute-start | bytes 2359304 | tf_op jit(solution)/shard_map/while/body/eval_jaxpr/ppermute | solution.py:13
  259.9 22.3 %collective-permute-start.2 = (s32[1,256]{1,0:T(1,128)S(1)}, s32[1,256]{1,0:T(1,128)S(1)}, u32[]{:S(2)}, u32[]{:S(2)}) collective-permute-start(s32[1,256]{1,0:T(1,128)S(1)} %get-tuple-element.367), channel_id=1, source_target_pairs={{0,16},{16,32},{32,48},{48,64},{64,80},{80,96},{96,112},{112,128},... | collective-permute-start | bytes 3080 | tf_op jit(solution)/shard_map/while/body/eval_jaxpr/ppermute | solution.py:13
  297.8 23.3 %collective-permute-start = (bf16[96,32,128]{2,1,0:T(8,128)(2,1)S(1)}, bf16[96,32,128]{2,1,0:T(8,128)(2,1)S(1)}, u32[]{:S(2)}, u32[]{:S(2)}) collective-permute-start(bf16[96,32,128]{2,1,0:T(8,128)(2,1)S(1)} %get-tuple-element.365), channel_id=1, source_target_pairs={{0,16},{16,32},{32,48},{48,64},{64,80},{80,96},{96,112},{112,128},... | collective-permute-start | bytes 2359304 | tf_op jit(solution)/shard_map/while/body/eval_jaxpr/ppermute | solution.py:13
  297.9 22.3 %collective-permute-start.2 = (s32[1,256]{1,0:T(1,128)S(1)}, s32[1,256]{1,0:T(1,128)S(1)}, u32[]{:S(2)}, u32[]{:S(2)}) collective-permute-start(s32[1,256]{1,0:T(1,128)S(1)} %get-tuple-element.367), channel_id=1, source_target_pairs={{0,16},{16,32},{32,48},{48,64},{64,80},{80,96},{96,112},{112,128},... | collective-permute-start | bytes 3080 | tf_op jit(solution)/shard_map/while/body/eval_jaxpr/ppermute | solution.py:13
  335.8 23.3 %collective-permute-start = (bf16[96,32,128]{2,1,0:T(8,128)(2,1)S(1)}, bf16[96,32,128]{2,1,0:T(8,128)(2,1)S(1)}, u32[]{:S(2)}, u32[]{:S(2)}) collective-permute-start(bf16[96,32,128]{2,1,0:T(8,128)(2,1)S(1)} %get-tuple-element.365), channel_id=1, source_target_pairs={{0,16},{16,32},{32,48},{48,64},{64,80},{80,96},{96,112},{112,128},... | collective-permute-start | bytes 2359304 | tf_op jit(solution)/shard_map/while/body/eval_jaxpr/ppermute | solution.py:13
  335.9 22.3 %collective-permute-start.2 = (s32[1,256]{1,0:T(1,128)S(1)}, s32[1,256]{1,0:T(1,128)S(1)}, u32[]{:S(2)}, u32[]{:S(2)}) collective-permute-start(s32[1,256]{1,0:T(1,128)S(1)} %get-tuple-element.367), channel_id=1, source_target_pairs={{0,16},{16,32},{32,48},{48,64},{64,80},{80,96},{96,112},{112,128},... | collective-permute-start | bytes 3080 | tf_op jit(solution)/shard_map/while/body/eval_jaxpr/ppermute | solution.py:13
  373.8 23.3 %collective-permute-start = (bf16[96,32,128]{2,1,0:T(8,128)(2,1)S(1)}, bf16[96,32,128]{2,1,0:T(8,128)(2,1)S(1)}, u32[]{:S(2)}, u32[]{:S(2)}) collective-permute-start(bf16[96,32,128]{2,1,0:T(8,128)(2,1)S(1)} %get-tuple-element.365), channel_id=1, source_target_pairs={{0,16},{16,32},{32,48},{48,64},{64,80},{80,96},{96,112},{112,128},... | collective-permute-start | bytes 2359304 | tf_op jit(solution)/shard_map/while/body/eval_jaxpr/ppermute | solution.py:13
  411.8 23.3 %collective-permute-start = (bf16[96,32,128]{2,1,0:T(8,128)(2,1)S(1)}, bf16[96,32,128]{2,1,0:T(8,128)(2,1)S(1)}, u32[]{:S(2)}, u32[]{:S(2)}) collective-permute-start(bf16[96,32,128]{2,1,0:T(8,128)(2,1)S(1)} %get-tuple-element.365), channel_id=1, source_target_pairs={{0,16},{16,32},{32,48},{48,64},{64,80},{80,96},{96,112},{112,128},... | collective-permute-start | bytes 2359304 | tf_op jit(solution)/shard_map/while/body/eval_jaxpr/ppermute | solution.py:13
  449.8 23.3 %collective-permute-start = (bf16[96,32,128]{2,1,0:T(8,128)(2,1)S(1)}, bf16[96,32,128]{2,1,0:T(8,128)(2,1)S(1)}, u32[]{:S(2)}, u32[]{:S(2)}) collective-permute-start(bf16[96,32,128]{2,1,0:T(8,128)(2,1)S(1)} %get-tuple-element.365), channel_id=1, source_target_pairs={{0,16},{16,32},{32,48},{48,64},{64,80},{80,96},{96,112},{112,128},... | collective-permute-start | bytes 2359304 | tf_op jit(solution)/shard_map/while/body/eval_jaxpr/ppermute | solution.py:13
  487.8 23.3 %collective-permute-start = (bf16[96,32,128]{2,1,0:T(8,128)(2,1)S(1)}, bf16[96,32,128]{2,1,0:T(8,128)(2,1)S(1)}, u32[]{:S(2)}, u32[]{:S(2)}) collective-permute-start(bf16[96,32,128]{2,1,0:T(8,128)(2,1)S(1)} %get-tuple-element.365), channel_id=1, source_target_pairs={{0,16},{16,32},{32,48},{48,64},{64,80},{80,96},{96,112},{112,128},... | collective-permute-start | bytes 2359304 | tf_op jit(solution)/shard_map/while/body/eval_jaxpr/ppermute | solution.py:13
  525.8 23.3 %collective-permute-start = (bf16[96,32,128]{2,1,0:T(8,128)(2,1)S(1)}, bf16[96,32,128]{2,1,0:T(8,128)(2,1)S(1)}, u32[]{:S(2)}, u32[]{:S(2)}) collective-permute-start(bf16[96,32,128]{2,1,0:T(8,128)(2,1)S(1)} %get-tuple-element.365), channel_id=1, source_target_pairs={{0,16},{16,32},{32,48},{48,64},{64,80},{80,96},{96,112},{112,128},... | collective-permute-start | bytes 2359304 | tf_op jit(solution)/shard_map/while/body/eval_jaxpr/ppermute | solution.py:13
  563.8 23.3 %collective-permute-start = (bf16[96,32,128]{2,1,0:T(8,128)(2,1)S(1)}, bf16[96,32,128]{2,1,0:T(8,128)(2,1)S(1)}, u32[]{:S(2)}, u32[]{:S(2)}) collective-permute-start(bf16[96,32,128]{2,1,0:T(8,128)(2,1)S(1)} %get-tuple-element.365), channel_id=1, source_target_pairs={{0,16},{16,32},{32,48},{48,64},{64,80},{80,96},{96,112},{112,128},... | collective-permute-start | bytes 2359304 | tf_op jit(solution)/shard_map/while/body/eval_jaxpr/ppermute | solution.py:13
  (40 other events, 1599.6 us)
where the time goes:
time: 605 us; the launch traced here: 603 us
  waiting for transfers between devices  409 us (68%)
  starting transfers between devices  87.5 us (14%)
  local copies, waits for them, and re-layouts  48.8 us (8%)
  matrix products  39.8 us (7%)
  other arithmetic  15.9 us (3%)
    ppermute x45, waiting for transfers between devices, passed_along(): lax.ppermute(x, axis, [(i, (i + by) % length) for i in range(length)])  317 us
    all_to_all x16, waiting for transfers between devices, gather_source(): lax.all_to_all(slices, 'grp', split_axis=0, concat_axis=0, tiled=True)  91.8 us
    all_to_all x16, starting transfers between devices, gather_source(): lax.all_to_all(slices, 'grp', split_axis=0, concat_axis=0, tiled=True)  77.4 us
    dot_general x16, matrix products, gather_source(): lax.dot_general(lax.all_to_all(slices, 'grp', split_axis=0, concat_axis=0...  19.9 us
    dot_general x16, matrix products, retarded(): jnp.einsum('mp,mpqr->mqr', weights, windows, precision=lax.Precision.HIGH...  15.5 us
    unnamed x10, local copies, waits for them, and re-layouts  14.5 us
  transfers between devices with their start and end apart: 61, of which 45 were waited for; matrix products, arithmetic and copies ran while one was open for 7% of the time, Pallas kernels for 0%

commit v1 on v0

v1 whole, which is shorter than its diff:
```python
import jax
import jax.numpy as jnp
import numpy as np
from jax import lax
from jax.experimental import pallas as pl
from jax.experimental.pallas import tpu as pltpu
from jax.sharding import PartitionSpec as P

ORDER = 4
FRAC = 8
HIST = 96
EXC = 32
ROWS = 128
NDEV = 256
NZ = 8
PLANE = 32
DZ = (4, 3, -3, 2, -2, 1, -1, 0)
GROUPS = 8
PER = PLANE // GROUPS
MESH = pl.DeviceIdType.MESH


def weight_table():
    fractions = np.arange(FRAC) / FRAC
    node_list = np.arange(ORDER) - (ORDER // 2 - 1)
    lagrange = np.ones((FRAC, ORDER))
    for column in range(ORDER):
        for partner in range(ORDER):
            if partner != column:
                lagrange[:, column] = (
                    lagrange[:, column]
                    * (fractions - node_list[partner])
                    / (node_list[column] - node_list[partner])
                )
    return lagrange.astype(np.float32)


def device_of(x, y, z, c):
    return (y // 2) * NZ + z, x * 4 + (y % 2) * 2 + c


def body(
    delays, offsets, history, kernel, incident, inverse, out,
    table, past, tiles, send, recv, load_sem, tile_sem, send_sem, recv_sem,
):
    blk = lax.axis_index("blk")
    grp = lax.axis_index("grp")
    z = blk % NZ
    x = grp // 4
    y = (blk // NZ) * 2 + (grp // 2) % 2
    c = grp % 2

    def shifted(r, dz, sign):
        dc = r % 2
        dy = (r // 2) % 4
        dx = r // 8
        return device_of(
            (x + sign * dx + 4) % 4,
            (y + sign * dy + 4) % 4,
            (z + sign * dz + NZ) % NZ,
            (c + dc) % 2,
        )

    load = pltpu.make_async_copy(history, past, load_sem)
    load.start()
    fetch = pltpu.make_async_copy(kernel, tiles, tile_sem)
    fetch.start()

    barrier = pltpu.get_barrier_semaphore()

    def unless_self(r, dz, act):
        if dz == 0:
            pl.when(r != 0)(act)
        else:
            act()

    def greet(r, carry):
        for dz in DZ:
            def act():
                pl.semaphore_signal(
                    barrier, inc=1, device_id=shifted(r, dz, 1), device_id_type=MESH
                )
            unless_self(r, dz, act)
        return carry

    lax.fori_loop(0, PLANE, greet, 0)

    weights = weight_table()
    for s in range(FRAC):
        for p in range(ORDER):
            table[s, p] = jnp.float32(weights[s, p])
    load.wait()

    def interpolate(r, carry):
        for k, dz in enumerate(DZ):
            there = shifted(r, dz, 1)
            to = there[0] * 16 + there[1]
            first = delays[0, to]
            part = offsets[0, to]
            total = table[part, 0] * past[first].astype(jnp.float32)
            for p in range(1, ORDER):
                total += table[part, p] * past[first + p].astype(jnp.float32)
            send[r * NZ + k] = total.astype(jnp.bfloat16)
        return carry

    lax.fori_loop(0, PLANE, interpolate, 0)
    own = len(DZ) - 1
    recv[own] = send[own]

    pl.semaphore_wait(barrier, NDEV - 1)

    def ship(r, carry):
        for k, dz in enumerate(DZ):
            def act():
                slot = r * NZ + k
                pltpu.make_async_remote_copy(
                    src_ref=send.at[slot],
                    dst_ref=recv.at[slot],
                    send_sem=send_sem,
                    recv_sem=recv_sem.at[r // PER],
                    device_id=shifted(r, dz, 1),
                    device_id_type=MESH,
                ).start()
            unless_self(r, dz, act)
        return carry

    lax.fori_loop(0, PLANE, ship, 0)
    fetch.wait()

    total = jnp.zeros((EXC, ROWS), jnp.float32)
    for group in range(GROUPS):
        count = PER * NZ - (1 if group == 0 else 0)
        span = recv.at[pl.ds(group * PER * NZ, count)]
        pltpu.make_async_copy(span, span, recv_sem.at[group]).wait()

        def gather(pair, carry):
            r = group * PER + pair * 2
            for k, dz in enumerate(DZ):
                low = recv[(r + c) * NZ + k]
                high = recv[(r + 1 - c) * NZ + k]
                there = shifted(r, dz, -1)
                column = pl.multiple_of((there[0] * 16 + there[1] - c) * ROWS, 2 * ROWS)
                carry += lax.dot_general(
                    jnp.concatenate([low, high], axis=1),
                    tiles[:, pl.ds(column, 2 * ROWS)],
                    (((1,), (1,)), ((), ())),
                    preferred_element_type=jnp.float32,
                )
            return carry

        total = lax.fori_loop(0, PER // 2, gather, total)

    rhs_field = incident[...] - total
    out[...] = lax.dot_general(
        rhs_field,
        inverse[...],
        (((1,), (1,)), ((), ())),
        precision=lax.Precision.HIGHEST,
        preferred_element_type=jnp.float32,
    )
    sent = send.at[pl.ds(0, NDEV - 1)]
    pltpu.make_async_copy(sent, sent, send_sem).wait()


def per_device(history, delays, offsets, kernel, incident, inverse):
    smem = pl.BlockSpec(memory_space=pltpu.SMEM)
    vmem = pl.BlockSpec(memory_space=pltpu.VMEM)
    hbm = pl.BlockSpec(memory_space=pltpu.HBM)
    return pl.pallas_call(
        body,
        name="retarded_exchange",
        out_shape=jax.ShapeDtypeStruct((EXC, ROWS), jnp.float32),
        in_specs=[smem, smem, hbm, hbm, vmem, vmem],
        out_specs=vmem,
        scratch_shapes=[
            pltpu.SMEM((FRAC, ORDER), jnp.float32),
            pltpu.VMEM((HIST, EXC, ROWS), jnp.bfloat16),
            pltpu.VMEM((ROWS, NDEV * ROWS), jnp.bfloat16),
            pltpu.VMEM((NDEV, EXC, ROWS), jnp.bfloat16),
            pltpu.VMEM((NDEV, EXC, ROWS), jnp.bfloat16),
            pltpu.SemaphoreType.DMA,
            pltpu.SemaphoreType.DMA,
            pltpu.SemaphoreType.DMA,
            pltpu.SemaphoreType.DMA((GROUPS,)),
        ],
        compiler_params=pltpu.CompilerParams(
            collective_id=0, has_side_effects=True, vmem_limit_bytes=60 << 20
        ),
    )(delays, offsets, history, kernel, incident, inverse)


def solution(mesh):
    return jax.shard_map(
        per_device,
        mesh=mesh,
        in_specs=(
            P(None, None, ("blk", "grp")),
            P(("blk", "grp"), None),
            P(("blk", "grp"), None),
            P(("blk", "grp"), None),
            P(None, ("blk", "grp")),
            P(("blk", "grp"), None),
        ),
        out_specs=P(None, ("blk", "grp")),
        check_vma=False,
    )
```

time: 605 us -> 67.5 us (0.11)
  waiting for transfers between devices: 409 us -> 0 us
  starting transfers between devices: 87.5 us -> 0 us
  Pallas kernels: 0 us -> 66 us
  local copies, waits for them, and re-layouts: 48.8 us -> 1.32 us
  matrix products: 39.8 us -> 0 us
  other arithmetic: 15.9 us -> 0 us
    ppermute x45 -> x0, waiting for transfers between devices: 317 us -> none  [passed_along(): lax.ppermute(x, axis, [(i, (i + by) % length) for i in range(length)])]
    all_to_all x16 -> x0, waiting for transfers between devices: 91.8 us -> none  [gather_source(): lax.all_to_all(slices, 'grp', split_axis=0, concat_axis=0, tiled=True)]
    all_to_all x16 -> x0, starting transfers between devices: 77.4 us -> none  [gather_source(): lax.all_to_all(slices, 'grp', split_axis=0, concat_axis=0, tiled=True)]
    pallas_call x0 -> x1, Pallas kernels: none -> 66 us  [per_device(): pl.pallas_call(body, name='retarded_exchange', out_shape=jax.ShapeDtypeSt...]
    dot_general x49 -> x0, matrix products: 39.8 us -> none  [the longest x16 19.9 us: gather_source(): lax.dot_general(lax.all_to_all(slices, 'grp', split_axis=0, concat_axis=0...]
    gather x48 -> x0, local copies, waits for them, and re-layouts: 31.9 us -> none  [the longest x16 10.7 us: retarded(): windows = jnp.take(history_block, window_rows, axis=0).astype(jnp.float32)]
    unnamed x10 -> x1, local copies, waits for them, and re-layouts: 14.5 us -> 1.32 us
    convert_element_type x16 -> x0, other arithmetic: 10.7 us -> none  [retarded(): return slices.astype(jnp.bfloat16)]
  transfers between devices with their start and end apart: 61 -> 0, of which waited for: 45 -> 0; matrix products, arithmetic and copies ran while one was open for 7% -> 0% of each run, Pallas kernels for 0% -> 0%
where the time goes in v1:
time: 67.5 us; the launch traced here: 67.3 us
  Pallas kernels  66 us (98%)
  local copies, waits for them, and re-layouts  1.32 us (2%)
    pallas_call x1, Pallas kernels, per_device(): pl.pallas_call(body, name='retarded_exchange', out_shape=jax.ShapeDtypeSt...  66 us

profile of v1, /device:TPU:1, one launch (start us, length us, event | category | flops | bytes accessed | tf_op | source)
XLA Modules:
  0.0 67.3 jit_solution(8729559926793148836)
XLA Ops:
  0.0 66.0 %retarded_exchange.1 = f32[32,128]{1,0:T(8,128)} custom-call(s32[1,256]{1,0:T(1,128)} %delays.1, s32[1,256]{1,0:T(1,128)} %offsets.1, bf16[96,32,128]{2,1,0:T(8,128)(2,1)} %history.1, bf16[128,32768]{1,0:T(8,128)(2,1)} %kernel.1, f32[32,128]{1,0:T(8,128)} %incident.1, f32[128,128]{1,0:T(8,128)} %inverse.1), custom_call_target="tpu_custom_call" | custom-call | tf_op jit(solution)/shard_map/retarded_exchange/pallas_call | solution.py:169
  66.0 1.3 %copy.8 = f32[32,128]{1,0:T(8,128)} copy(f32[32,128]{1,0:T(8,128)} %retarded_exchange.1) | data formatting | bytes 32768

commit v2 on v1

v2 whole, which is shorter than its diff:
```python
import jax
import jax.numpy as jnp
import numpy as np
from jax import lax
from jax.experimental import pallas as pl
from jax.experimental.pallas import tpu as pltpu
from jax.sharding import PartitionSpec as P

ORDER = 4
FRAC = 8
HIST = 96
EXC = 32
ROWS = 128
NDEV = 256
NX = 4
NY = 4
NZ = 8
MESH = pl.DeviceIdType.MESH


def hops(dx, dy, dz):
    return min(dx, NX - dx) + min(dy, NY - dy) + min(dz, NZ - dz)


PLANE = sorted(((dx, dy) for dx in range(NX) for dy in range(NY)), key=lambda d: hops(*d, 0))
CHIPS = [(dx, dy, dz) for dx, dy in PLANE for dz in range(NZ)]
FARTHEST = max(hops(*d) for d in CHIPS)
BY_HOPS = [
    sorted((d for d in CHIPS if hops(*d) == far), key=lambda d: -min(d[2], NZ - d[2]))
    for far in range(FARTHEST + 1)
]
SLOT = {d: 2 * n for n, d in enumerate(sum(BY_HOPS, []))}
GROUPS = ((0, 1), (2,), (3,), (4,), (5,), (6,), (7, 8))
GROUP_OF = {far: n for n, group in enumerate(GROUPS) for far in group}
PARTS = ((0, 1), (2,), (3, 4))
NEXT = ((1, 0, 0), (3, 0, 0), (0, 1, 0), (0, 3, 0), (0, 0, 1), (0, 0, 7))


def weight_table():
    fractions = np.arange(FRAC) / FRAC
    node_list = np.arange(ORDER) - (ORDER // 2 - 1)
    lagrange = np.ones((FRAC, ORDER))
    for column in range(ORDER):
        for partner in range(ORDER):
            if partner != column:
                lagrange[:, column] = (
                    lagrange[:, column]
                    * (fractions - node_list[partner])
                    / (node_list[column] - node_list[partner])
                )
    return lagrange.astype(np.float32)


def body(
    delays, offsets, history, kernel, incident, inverse, out,
    late, part_of, table, past, tiles, field, solve, send, recv,
    load_sem, send_sem, recv_sem, known_sem,
):
    blk = lax.axis_index("blk")
    grp = lax.axis_index("grp")
    z = blk % NZ
    x = grp // 4
    y = (blk // NZ) * 2 + (grp // 2) % 2
    c = grp % 2

    at_x = [((x + d) % NX) * 4 for d in range(NX)]
    ys = [(y + d) % NY for d in range(NY)]
    at_y = [((v // 2) * NZ, (v % 2) * 2) for v in ys]
    at_z = [(z + d) % NZ for d in range(NZ)]
    at_c = [c, 1 - c]

    def device(dx, dy, dz, dc):
        return at_y[dy][0] + at_z[dz], at_x[dx] + at_y[dy][1] + at_c[dc]

    def source_chip(dx, dy, dz):
        there = device(-dx % NX, -dy % NY, -dz % NZ, 0)
        return there[0] * 16 + there[1] - c

    def tell(sem, place):
        pl.semaphore_signal(sem, inc=1, device_id=device(*place), device_id_type=MESH)

    barrier = pltpu.get_barrier_semaphore()
    tell(barrier, (0, 0, 0, 1))
    for chip in NEXT:
        for dc in range(2):
            tell(barrier, (*chip, dc))

    loads = [
        pltpu.make_async_copy(source, target, load_sem.at[n])
        for n, (source, target) in enumerate(
            (
                (delays, late),
                (offsets, part_of),
                (history, past),
                (kernel, tiles),
                (incident, field),
                (inverse, solve),
            )
        )
    ]
    for load in loads:
        load.start()
    weights = weight_table()
    for s in range(FRAC):
        for p in range(ORDER):
            table[s, p] = jnp.float32(weights[s, p])
    for load in loads[:3]:
        load.wait()

    def interpolate(distances):
        plane = [d for d in PLANE if hops(*d, 0) in distances]

        def one_layer(dz, carry):
            for dx, dy in plane:
                for dc in range(2):
                    to = (at_y[dy][0] + (z + dz) % NZ) * 16 + at_x[dx] + at_y[dy][1] + at_c[dc]
                    first = late[0, to]
                    part = part_of[0, to]
                    total = table[part, 0] * past[first].astype(jnp.float32)
                    for p in range(1, ORDER):
                        total += table[part, p] * past[first + p].astype(jnp.float32)
                    send[((PLANE.index((dx, dy)) * NZ) + dz) * 2 + dc] = total.astype(jnp.bfloat16)
            return carry

        lax.fori_loop(0, NZ, one_layer, 0)

    def ship(far):
        for chip in BY_HOPS[far]:
            for dc in range(2):
                if (*chip, dc) == (0, 0, 0, 0):
                    continue
                start = (PLANE.index(chip[:2]) * NZ + chip[2]) * 2 + dc
                pltpu.make_async_remote_copy(
                    src_ref=send.at[start],
                    dst_ref=recv.at[SLOT[chip] + dc],
                    send_sem=send_sem,
                    recv_sem=recv_sem.at[GROUP_OF[far]],
                    device_id=device(*chip, dc),
                    device_id_type=MESH,
                ).start()

    for far in range(1, FARTHEST + 1):
        if far <= len(PARTS):
            interpolate(PARTS[far - 1])
        if far == 1:
            recv[SLOT[0, 0, 0]] = send[0]
            pl.semaphore_wait(barrier, 2 * len(NEXT) + 1)
        else:
            pl.semaphore_wait(known_sem.at[far], len(NEXT))
        if far < FARTHEST:
            for chip in NEXT:
                tell(known_sem.at[far + 1], (*chip, 0))
        if far == 1:
            ship(0)
        ship(far)

    for load in loads[3:]:
        load.wait()

    total = jnp.zeros((EXC, ROWS), jnp.float32)
    for n, group in enumerate(GROUPS):
        chips = [d for far in group for d in BY_HOPS[far]]
        count = 2 * len(chips) - (1 if 0 in group else 0)
        span = recv.at[pl.ds(SLOT[chips[0]] + (1 if 0 in group else 0), count)]
        pltpu.make_async_copy(span, span, recv_sem.at[n]).wait()
        for chip in chips:
            low = recv[SLOT[chip] + c]
            high = recv[SLOT[chip] + 1 - c]
            column = pl.multiple_of(source_chip(*chip) * ROWS, 2 * ROWS)
            total += lax.dot_general(
                jnp.concatenate([low, high], axis=1),
                tiles[:, pl.ds(column, 2 * ROWS)],
                (((1,), (1,)), ((), ())),
                preferred_element_type=jnp.float32,
            )

    out[...] = lax.dot_general(
        field[...] - total,
        solve[...],
        (((1,), (1,)), ((), ())),
        precision=lax.Precision.HIGHEST,
        preferred_element_type=jnp.float32,
    )
    sent = send.at[pl.ds(1, NDEV - 1)]
    pltpu.make_async_copy(sent, sent, send_sem).wait()


def per_device(history, delays, offsets, kernel, incident, inverse):
    hbm = pl.BlockSpec(memory_space=pltpu.HBM)
    return pl.pallas_call(
        body,
        name="retarded_exchange",
        out_shape=jax.ShapeDtypeStruct((EXC, ROWS), jnp.float32),
        in_specs=[hbm] * 6,
        out_specs=pl.BlockSpec(memory_space=pltpu.VMEM),
        scratch_shapes=[
            pltpu.SMEM((1, NDEV), jnp.int32),
            pltpu.SMEM((1, NDEV), jnp.int32),
            pltpu.SMEM((FRAC, ORDER), jnp.float32),
            pltpu.VMEM((HIST, EXC, ROWS), jnp.bfloat16),
            pltpu.VMEM((ROWS, NDEV * ROWS), jnp.bfloat16),
            pltpu.VMEM((EXC, ROWS), jnp.float32),
            pltpu.VMEM((ROWS, ROWS), jnp.float32),
            pltpu.VMEM((NDEV, EXC, ROWS), jnp.bfloat16),
            pltpu.VMEM((NDEV, EXC, ROWS), jnp.bfloat16),
            pltpu.SemaphoreType.DMA((6,)),
            pltpu.SemaphoreType.DMA,
            pltpu.SemaphoreType.DMA((len(GROUPS),)),
            pltpu.SemaphoreType.REGULAR((FARTHEST + 1,)),
        ],
        compiler_params=pltpu.CompilerParams(
            collective_id=0, has_side_effects=True, vmem_limit_bytes=60 << 20
        ),
    )(delays, offsets, history, kernel, incident, inverse)


def solution(mesh):
    return jax.shard_map(
        per_device,
        mesh=mesh,
        in_specs=(
            P(None, None, ("blk", "grp")),
            P(("blk", "grp"), None),
            P(("blk", "grp"), None),
            P(("blk", "grp"), None),
            P(None, ("blk", "grp")),
            P(("blk", "grp"), None),
        ),
        out_specs=P(None, ("blk", "grp")),
        check_vma=False,
    )
```

time: 67.5 us -> 63.4 us (0.939)
  Pallas kernels: 66 us -> 61.9 us
    pallas_call x1, Pallas kernels: 66 us -> 61.9 us  [per_device(): pl.pallas_call(body, name='retarded_exchange', out_shape=jax.ShapeDtypeSt...]
where the time goes in v2:
time: 63.4 us; the launch traced here: 63.2 us
  Pallas kernels  61.9 us (98%)
  local copies, waits for them, and re-layouts  1.32 us (2%)
    pallas_call x1, Pallas kernels, per_device(): pl.pallas_call(body, name='retarded_exchange', out_shape=jax.ShapeDtypeSt...  61.9 us
    unnamed x1, local copies, waits for them, and re-layouts  1.32 us

profile of v2, /device:TPU:1, one launch (start us, length us, event | category | flops | bytes accessed | tf_op | source)
XLA Modules:
  0.0 63.2 jit_solution(5608821036593110635)
XLA Ops:
  0.0 61.9 %retarded_exchange.1 = f32[32,128]{1,0:T(8,128)} custom-call(s32[1,256]{1,0:T(1,128)} %delays.1, s32[1,256]{1,0:T(1,128)} %offsets.1, bf16[96,32,128]{2,1,0:T(8,128)(2,1)} %history.1, bf16[128,32768]{1,0:T(8,128)(2,1)} %kernel.1, f32[32,128]{1,0:T(8,128)} %incident.1, f32[128,128]{1,0:T(8,128)} %inverse.1), custom_call_target="tpu_custom_call" | custom-call | tf_op jit(solution)/shard_map/retarded_exchange/pallas_call | solution.py:190
  61.9 1.3 %copy.8 = f32[32,128]{1,0:T(8,128)} copy(f32[32,128]{1,0:T(8,128)} %retarded_exchange.1) | data formatting | bytes 32768

commit v3 on v2

--- a/solution.py
+++ b/solution.py
@@ -25,15 +25,28 @@
 PLANE = sorted(((dx, dy) for dx in range(NX) for dy in range(NY)), key=lambda d: hops(*d, 0))
 CHIPS = [(dx, dy, dz) for dx, dy in PLANE for dz in range(NZ)]
 FARTHEST = max(hops(*d) for d in CHIPS)
-BY_HOPS = [
-    sorted((d for d in CHIPS if hops(*d) == far), key=lambda d: -min(d[2], NZ - d[2]))
-    for far in range(FARTHEST + 1)
-]
-SLOT = {d: 2 * n for n, d in enumerate(sum(BY_HOPS, []))}
-GROUPS = ((0, 1), (2,), (3,), (4,), (5,), (6,), (7, 8))
-GROUP_OF = {far: n for n, group in enumerate(GROUPS) for far in group}
+def make_plan():
+    def long_way(d):
+        return min(d[2], NZ - d[2])
+
+    def ring(far, sign):
+        return sorted((d for d in CHIPS if hops(*d) == far), key=lambda d: sign * long_way(d))
+
+    return [ring(0, 1) + ring(1, -1), ring(2, -1), ring(3, 1) + ring(4, 1), ring(5, 1) + ring(6, 1) + ring(7, 1) + ring(8, 1)]
+
+
+LEAD = (2, 4)
+NEXT = ((1, 0, 0), (3, 0, 0), (0, 1, 0), (0, 3, 0), (0, 0, 1), (0, 0, 7))
+TELLERS = (NEXT, NEXT, tuple(d for d in CHIPS if hops(*d) == 2), ((2, 2, 0), (0, 0, 4)))
+PLAN = make_plan()
+ORDERED = sum(PLAN, [])
+assert sorted(ORDERED) == sorted(CHIPS)
+SLOT = {d: 2 * n for n, d in enumerate(ORDERED)}
+SIZES = (8, 20, 24, 24, 24, 16, 8, 4)
+ENDS = [sum(SIZES[:n + 1]) for n in range(len(SIZES))]
+GROUPS = [ORDERED[end - size:end] for size, end in zip(SIZES, ENDS)]
+GROUP_OF = {d: n for n, group in enumerate(GROUPS) for d in group}
 PARTS = ((0, 1), (2,), (3, 4))
-NEXT = ((1, 0, 0), (3, 0, 0), (0, 1, 0), (0, 3, 0), (0, 0, 1), (0, 0, 7))
 
 
 def weight_table():
@@ -124,44 +137,64 @@
 
         lax.fori_loop(0, NZ, one_layer, 0)
 
-    def ship(far):
-        for chip in BY_HOPS[far]:
-            for dc in range(2):
-                if (*chip, dc) == (0, 0, 0, 0):
-                    continue
-                start = (PLANE.index(chip[:2]) * NZ + chip[2]) * 2 + dc
-                pltpu.make_async_remote_copy(
-                    src_ref=send.at[start],
-                    dst_ref=recv.at[SLOT[chip] + dc],
-                    send_sem=send_sem,
-                    recv_sem=recv_sem.at[GROUP_OF[far]],
-                    device_id=device(*chip, dc),
-                    device_id_type=MESH,
-                ).start()
-
-    for far in range(1, FARTHEST + 1):
-        if far <= len(PARTS):
-            interpolate(PARTS[far - 1])
-        if far == 1:
+    lead_x = [jnp.minimum((x + d) % NX, 2) for d in range(NX)]
+    lead_y = [jnp.minimum(v, 2) for v in ys]
+    lead_z = [v + NZ * (v // 4) for v in at_z]
+
+    def send_to(chip):
+        for dc in range(2):
+            if (*chip, dc) == (0, 0, 0, 0):
+                continue
+            start = (PLANE.index(chip[:2]) * NZ + chip[2]) * 2 + dc
+            pltpu.make_async_remote_copy(
+                src_ref=send.at[start],
+                dst_ref=recv.at[SLOT[chip] + dc],
+                send_sem=send_sem,
+                recv_sem=recv_sem.at[GROUP_OF[chip]],
+                device_id=device(*chip, dc),
+                device_id_type=MESH,
+            ).start()
+
+    def ship(stage):
+        if stage + 1 < len(PLAN):
+            for chip in PLAN[stage]:
+                send_to(chip)
+            return
+        for tier in range(len(LEAD) + 1):
+            for chip in PLAN[stage]:
+                dx, dy, dz = chip
+                lead = lead_x[dx] + lead_y[dy] + lead_z[dz]
+                if tier == 0:
+                    ahead = lead <= LEAD[0]
+                elif tier == len(LEAD):
+                    ahead = lead > LEAD[-1]
+                else:
+                    ahead = jnp.logical_and(lead > LEAD[tier - 1], lead <= LEAD[tier])
+
+                @pl.when(ahead)
+                def _():
+                    send_to(chip)
+
+    for stage, tellers in enumerate(TELLERS):
+        if stage < len(PARTS):
+            interpolate(PARTS[stage])
+        if stage == 0:
             recv[SLOT[0, 0, 0]] = send[0]
             pl.semaphore_wait(barrier, 2 * len(NEXT) + 1)
         else:
-            pl.semaphore_wait(known_sem.at[far], len(NEXT))
-        if far < FARTHEST:
-            for chip in NEXT:
-                tell(known_sem.at[far + 1], (*chip, 0))
-        if far == 1:
-            ship(0)
-        ship(far)
+            pl.semaphore_wait(known_sem.at[stage], len(tellers))
+        if stage + 1 < len(TELLERS):
+            for chip in TELLERS[stage + 1]:
+                tell(known_sem.at[stage + 1], (*chip, 0))
+        ship(stage)
 
     for load in loads[3:]:
         load.wait()
 
     total = jnp.zeros((EXC, ROWS), jnp.float32)
-    for n, group in enumerate(GROUPS):
-        chips = [d for far in group for d in BY_HOPS[far]]
-        count = 2 * len(chips) - (1 if 0 in group else 0)
-        span = recv.at[pl.ds(SLOT[chips[0]] + (1 if 0 in group else 0), count)]
+    for n, chips in enumerate(GROUPS):
+        own = 1 if (0, 0, 0) in chips else 0
+        span = recv.at[pl.ds(SLOT[chips[0]] + own, 2 * len(chips) - own)]
         pltpu.make_async_copy(span, span, recv_sem.at[n]).wait()
         for chip in chips:
             low = recv[SLOT[chip] + c]
@@ -206,7 +239,7 @@
             pltpu.SemaphoreType.DMA((6,)),
             pltpu.SemaphoreType.DMA,
             pltpu.SemaphoreType.DMA((len(GROUPS),)),
-            pltpu.SemaphoreType.REGULAR((FARTHEST + 1,)),
+            pltpu.SemaphoreType.REGULAR((len(TELLERS),)),
         ],
         compiler_params=pltpu.CompilerParams(
             collective_id=0, has_side_effects=True, vmem_limit_bytes=60 << 20

time: 63.4 us -> 60 us (0.946)
  the two profiles are of different devices: /device:TPU:1 before, /device:TPU:101 now
where the time goes in v3:
time: 60 us; the launch traced here: 59.8 us
  Pallas kernels  58.5 us (98%)
  local copies, waits for them, and re-layouts  1.32 us (2%)
    pallas_call x1, Pallas kernels, per_device(): pl.pallas_call(body, name='retarded_exchange', out_shape=jax.ShapeDtypeSt...  58.5 us
    unnamed x1, local copies, waits for them, and re-layouts  1.32 us

profile of v3, /device:TPU:101, one launch (start us, length us, event | category | flops | bytes accessed | tf_op | source)
XLA Modules:
  0.0 59.8 jit_solution(5062825812232036575)
XLA Ops:
  0.0 58.5 %retarded_exchange.1 = f32[32,128]{1,0:T(8,128)} custom-call(s32[1,256]{1,0:T(1,128)} %delays.1, s32[1,256]{1,0:T(1,128)} %offsets.1, bf16[96,32,128]{2,1,0:T(8,128)(2,1)} %history.1, bf16[128,32768]{1,0:T(8,128)(2,1)} %kernel.1, f32[32,128]{1,0:T(8,128)} %incident.1, f32[128,128]{1,0:T(8,128)} %inverse.1), custom_call_target="tpu_custom_call" | custom-call | tf_op jit(solution)/shard_map/retarded_exchange/pallas_call | solution.py:223
  58.5 1.3 %copy.8 = f32[32,128]{1,0:T(8,128)} copy(f32[32,128]{1,0:T(8,128)} %retarded_exchange.1) | data formatting | bytes 32768

commit v4 on v3

--- a/solution.py
+++ b/solution.py
@@ -220,6 +220,10 @@
 
 def per_device(history, delays, offsets, kernel, incident, inverse):
     hbm = pl.BlockSpec(memory_space=pltpu.HBM)
+    args = [
+        pltpu.with_memory_space_constraint(a, pltpu.HBM)
+        for a in (delays, offsets, history, kernel, incident, inverse)
+    ]
     return pl.pallas_call(
         body,
         name="retarded_exchange",
@@ -242,9 +246,9 @@
             pltpu.SemaphoreType.REGULAR((len(TELLERS),)),
         ],
         compiler_params=pltpu.CompilerParams(
-            collective_id=0, has_side_effects=True, vmem_limit_bytes=60 << 20
+            collective_id=0, has_side_effects=True, vmem_limit_bytes=40 << 20
         ),
-    )(delays, offsets, history, kernel, incident, inverse)
+    )(*args)
 
 
 def solution(mesh):

time: 60 us -> 58.6 us (0.977)
  local copies, waits for them, and re-layouts: 1.32 us -> 0.61 us
  Pallas kernels: 58.5 us -> 57.9 us
    unnamed x1, local copies, waits for them, and re-layouts: 1.32 us -> 0.61 us
    pallas_call x1, Pallas kernels: 58.5 us -> 57.9 us  [per_device(): pl.pallas_call(body, name='retarded_exchange', out_shape=jax.ShapeDtypeSt...]
where the time goes in v4:
time: 58.6 us; the launch traced here: 58.5 us
  Pallas kernels  57.9 us (99%)
  local copies, waits for them, and re-layouts  0.61 us (1%)
    pallas_call x1, Pallas kernels, per_device(): pl.pallas_call(body, name='retarded_exchange', out_shape=jax.ShapeDtypeSt...  57.9 us

profile of v4, /device:TPU:101, one launch (start us, length us, event | category | flops | bytes accessed | tf_op | source)
XLA Modules:
  0.0 58.5 jit_solution(6978686862311172520)
XLA Ops:
  0.0 57.9 %retarded_exchange.1 = f32[32,128]{1,0:T(8,128)S(1)} custom-call(s32[1,256]{1,0:T(1,128)} %delays.1, s32[1,256]{1,0:T(1,128)} %offsets.1, bf16[96,32,128]{2,1,0:T(8,128)(2,1)} %history.1, bf16[128,32768]{1,0:T(8,128)(2,1)} %kernel.1, f32[32,128]{1,0:T(8,128)} %incident.1, f32[128,128]{1,0:T(8,128)} %inverse.1), custom_call_target="tpu_custom_call" | custom-call | tf_op jit(solution)/shard_map/retarded_exchange/pallas_call | solution.py:227
  57.9 0.6 %copy.8 = f32[32,128]{1,0:T(8,128)} copy(f32[32,128]{1,0:T(8,128)S(1)} %retarded_exchange.1) | data formatting | bytes 32768

commit v5 on v4

--- a/solution.py
+++ b/solution.py
@@ -32,10 +32,10 @@
     def ring(far, sign):
         return sorted((d for d in CHIPS if hops(*d) == far), key=lambda d: sign * long_way(d))
 
-    return [ring(0, 1) + ring(1, -1), ring(2, -1), ring(3, 1) + ring(4, 1), ring(5, 1) + ring(6, 1) + ring(7, 1) + ring(8, 1)]
-
-
-LEAD = (2, 4)
+    return [ring(0, 1) + ring(1, -1), ring(2, -1), ring(3, 1) + ring(4, 1)[:14], ring(4, 1)[14:] + ring(5, 1) + ring(6, 1) + ring(7, 1) + ring(8, 1)]
+
+
+LEAD = (2, 3, 4)
 NEXT = ((1, 0, 0), (3, 0, 0), (0, 1, 0), (0, 3, 0), (0, 0, 1), (0, 0, 7))
 TELLERS = (NEXT, NEXT, tuple(d for d in CHIPS if hops(*d) == 2), ((2, 2, 0), (0, 0, 4)))
 PLAN = make_plan()

time: 58.6 us -> 58.6 us (level)
  no operation moved by 1% of the time
where the time goes in v5:
time: 58.6 us; the launch traced here: 58.5 us
  Pallas kernels  57.9 us (99%)
  local copies, waits for them, and re-layouts  0.61 us (1%)
    pallas_call x1, Pallas kernels, per_device(): pl.pallas_call(body, name='retarded_exchange', out_shape=jax.ShapeDtypeSt...  57.9 us

profile of v5, /device:TPU:101, one launch (start us, length us, event | category | flops | bytes accessed | tf_op | source)
XLA Modules:
  0.0 58.5 jit_solution(8657017323394650713)
XLA Ops:
  0.0 57.9 %retarded_exchange.1 = f32[32,128]{1,0:T(8,128)S(1)} custom-call(s32[1,256]{1,0:T(1,128)} %delays.1, s32[1,256]{1,0:T(1,128)} %offsets.1, bf16[96,32,128]{2,1,0:T(8,128)(2,1)} %history.1, bf16[128,32768]{1,0:T(8,128)(2,1)} %kernel.1, f32[32,128]{1,0:T(8,128)} %incident.1, f32[128,128]{1,0:T(8,128)} %inverse.1), custom_call_target="tpu_custom_call" | custom-call | tf_op jit(solution)/shard_map/retarded_exchange/pallas_call | solution.py:227
  57.9 0.6 %copy.8 = f32[32,128]{1,0:T(8,128)} copy(f32[32,128]{1,0:T(8,128)S(1)} %retarded_exchange.1) | data formatting | bytes 32768
